TPU v7x, 512 devices: a whole 4x8x8 slice. The times are simulated.
512 devices in a mesh: dp: 32 (over z, x_hi, core), fsdp: 16 (over x_lo, y).
Axes of the slice: x: 4 (x_hi: 2, x_lo: 2; x = x_hi * 2 + x_lo), y: 8, z: 8, core: 2. Of those that a mesh axis runs over, the one named last changes fastest.
Arguments:
- activations: bfloat16 [98304, 4096], P(('dp', 'fsdp')), may hold values from -24 to 24
- cotangent: bfloat16 [98304, 512], P(('dp', 'fsdp')), may hold values from -6 to 6
- weight: bfloat16 [4096, 512], P('fsdp'), may hold values from -0.09375 to 0.09375
- momentum: float32 [32, 4096, 512], P('dp', 'fsdp'), may hold values from -256 to 256
- positions: int32 [16, 32, 512], P('fsdp'), may hold values from 0 to 255, as said below
Outputs:
- grad_input: bfloat16 [98304, 4096], P(('dp', 'fsdp'))
- new_momentum: float32 [32, 4096, 512], P('dp', 'fsdp')
- update: bfloat16 [4096, 512], P('fsdp')
Inputs may be any that keep to these rules, and one draw needn't show every extreme that they name: For each block b and column c the 32 values positions[b, :, c] are distinct.
All inputs are finite; a program needn't handle non-finite values.
Results may differ from a plain program's by a relative error of at most 0.023.
Values may be sent and summed in bfloat16 or wider, within the bound.
A program may use at most 64 MiB of HBM per device.

v0:
```python
import math

import jax
import jax.numpy as jnp
from jax import lax
from jax.sharding import PartitionSpec as P

SPAN = 256


MOMENTUM_DECAY = 0.999


def transform_table(length):
    freq = jnp.arange(length, dtype=jnp.float32)[:, None]
    place = jnp.arange(length, dtype=jnp.float32)[None, :]
    angles = jnp.pi * (2.0 * place + 1.0) * freq / (2.0 * length)
    scales = jnp.where(freq == 0.0, jnp.sqrt(1.0 / length), jnp.sqrt(2.0 / length))
    return scales * jnp.cos(angles)


def forward_blocks(table, blocks):
    return jnp.einsum("kn,bnc->bkc", table, blocks, precision=lax.Precision.HIGHEST)


def inverse_blocks(table, coeffs):
    return jnp.einsum("kn,bkc->bnc", table, coeffs, precision=lax.Precision.HIGHEST)


def grouped_positions(positions):
    blocks, picks, columns = positions.shape
    group = math.gcd(picks, 8)
    stacked = positions.reshape(blocks, picks // group, group, columns)
    return (jnp.transpose(stacked, (1, 0, 2, 3)), group)


def pick_band(coeffs, positions):
    blocks, length, columns = coeffs.shape
    picks = positions.shape[1]
    stacked, group = grouped_positions(positions)
    levels = jnp.arange(length, dtype=jnp.int32)[None, None, :, None]

    def one_group(where):
        onehot = where[:, :, None, :] == levels
        return jnp.sum(jnp.where(onehot, coeffs[:, None, :, :], 0.0), axis=2)

    found = lax.map(one_group, stacked)
    return jnp.transpose(found, (1, 0, 2, 3)).reshape(blocks, picks, columns)


def place_band(values, positions, length):
    blocks, picks, columns = values.shape
    stacked, group = grouped_positions(positions)
    stacked_values = jnp.transpose(
        values.reshape(blocks, picks // group, group, columns), (1, 0, 2, 3)
    )
    levels = jnp.arange(length, dtype=jnp.int32)[None, None, :, None]

    def add_group(dense, packed):
        where, amounts = packed
        onehot = where[:, :, None, :] == levels
        return (dense + jnp.sum(jnp.where(onehot, amounts[:, :, None, :], 0.0), axis=1), None)

    start = jnp.zeros((blocks, length, columns), jnp.float32)
    dense, unused = lax.scan(add_group, start, (stacked, stacked_values))
    return dense


def contract_last(left, right):
    return lax.dot_general(
        left, right, (((1,), (1,)), ((), ())), preferred_element_type=jnp.float32
    )


def on_device(activations, cotangent, weight, momentum, positions):
    table = transform_table(SPAN)
    grad_input = contract_last(
        cotangent, lax.all_gather(weight, "fsdp", axis=0, tiled=True)
    ).astype(jnp.bfloat16)
    gradient = lax.psum_scatter(
        lax.dot_general(
            activations, cotangent, (((0,), (0,)), ((), ())), preferred_element_type=jnp.float32
        ).astype(jnp.bfloat16),
        "fsdp",
        scatter_dimension=0,
        tiled=True,
    ).astype(jnp.float32)
    moment = MOMENTUM_DECAY * momentum[0] + gradient
    blocks = moment.reshape(positions.shape[0], SPAN, moment.shape[1])
    coeffs = forward_blocks(table, blocks)
    picked = pick_band(coeffs, positions)
    kept = blocks - inverse_blocks(table, place_band(picked, positions, SPAN))
    new_momentum = kept.reshape(moment.shape)[None]
    bands = picked.astype(jnp.bfloat16)
    replicas = lax.axis_size("dp")
    summed = jnp.sum(
        lax.all_gather(bands[None], "dp", axis=0, tiled=True).astype(jnp.float32), axis=0
    )
    mean_band = summed / replicas
    update = (
        inverse_blocks(table, place_band(mean_band, positions, SPAN))
        .reshape(moment.shape)
        .astype(jnp.bfloat16)
    )
    return (grad_input, new_momentum, update)


def solution(mesh):
    placed = (
        P(("dp", "fsdp"), None),
        P(("dp", "fsdp"), None),
        P("fsdp", None),
        P("dp", "fsdp", None),
        P("fsdp", None, None),
    )
    return jax.shard_map(
        on_device,
        mesh=mesh,
        in_specs=placed,
        out_specs=(P(("dp", "fsdp"), None), P("dp", "fsdp", None), P("fsdp", None)),
        check_vma=False,
    )
```

profile of v0, /device:TPU:1, one launch (start us, length us, event | category | flops | bytes accessed | tf_op | source)
XLA Modules:
  0.0 280.2 jit_solution(7000928409608363338)
XLA Ops:
  7.2 0.0 copy-start
  7.2 0.0 all-gather.3.cloned.1.call-start
  7.2 0.7 all-gather.3.cloned.1.call-update
  7.9 0.0 reduce-scatter.2.cloned.1.call-start
  8.0 0.6 copy-done
  8.6 4.2 %convolution_convert_fusion = bf16[4096,512]{1,0:T(8,128)(2,1)} fusion(bf16[192,4096]{1,0:T(8,128)(2,1)S(1)} %copy-done, bf16[192,512]{1,0:T(8,128)(2,1)} %param.12), kind=kOutput, calls=%fused_computation.17 | convolution fusion | flops 807403520 | bytes 5963776 | tf_op jit(solution)/shard_map/dot_general | solution.py:81
  12.8 0.0 reduce-scatter.2.cloned.1.call-update
  12.8 0.0 copy-start.3
  12.8 0.0 all-gather.5.cloned.1.call-start
  12.9 73.1 %all-gather.3.cloned.1.call-done = bf16[4096,512]{1,0:T(8,128)(2,1)} async-done(((bf16[256,512]{1,0:T(8,128)(2,1)}), bf16[4096,512]{1,0:T(8,128)(2,1)}) %all-gather.3.cloned.1.call-update) | async-done | bytes 4194320 | tf_op jit(solution)/shard_map/all_gather | solution.py:78
  86.0 0.0 copy-done.4
  86.0 4.8 %convolution_convert_fusion.1 = bf16[192,4096]{1,0:T(8,128)(2,1)} fusion(bf16[192,512]{1,0:T(8,128)(2,1)S(1)} %copy-done.4, bf16[4096,512]{1,0:T(8,128)(2,1)} %all-gather.3.cloned.1.call-done), kind=kOutput, calls=%fused_computation.18 | convolution fusion | flops 806092800 | bytes 5963776 | tf_op jit(solution)/shard_map/dot_general | solution.py:70
  90.9 77.3 %reduce-scatter.2.cloned.1.call-done = bf16[256,512]{1,0:T(8,128)(2,1)} async-done(((bf16[4096,512]{1,0:T(8,128)(2,1)}), bf16[256,512]{1,0:T(8,128)(2,1)}) %reduce-scatter.2.cloned.1.call-update) | async-done | bytes 262160 | tf_op jit(solution)/shard_map/reduce_scatter | solution.py:80
  168.2 0.0 copy-done.1
  168.2 3.6 %convolution_bitcast_fusion.1 = f32[1,256,512]{1,2,0:T(8,128)} fusion(bf16[256,512]{1,0:T(8,128)(2,1)} %reduce-scatter.2.cloned.1.call-done, f32[1,256,512]{2,1,0:T(8,128)S(1)} %copy-done.1, f32[256]{0:T(256)S(1)} %get-tuple-element.184, f32[256]{0:T(256)S(1)} %get-tuple-element.183), kind=kOutput, calls=%fused_computation.21 | convolution fusion | flops 403243008 | bytes 1312768 | tf_op jit(solution)/shard_map/kn,bnc->bkc/dot_general | solution.py:23
  171.8 1.2 copy.17
  173.1 2.1 while.33
  173.1 0.5 select_reduce_fusion.6
  173.6 0.5 select_reduce_fusion.6
  174.1 0.5 select_reduce_fusion.6
  174.7 0.5 select_reduce_fusion.6
  175.2 0.6 convert_bitcast_fusion
  175.8 0.0 all-gather.5.cloned.1.call-update
  175.8 0.0 copy-start.2
  175.8 3.1 %while.34 = (s32[]{:T(128)}, f32[1,256,512]{2,1,0:T(8,128)S(1)}, s32[4,1,8,512]{3,2,1,0:T(8,128)S(1)}, f32[4,1,8,512]{3,2,1,0:T(8,128)S(1)}, s32[]{:T(128)}, /*index=5*/s32[]{:T(128)}) while((s32[]{:T(128)}, f32[1,256,512]{2,1,0:T(8,128)S(1)}, s32[4,1,8,512]{3,2,1,0:T(8,128)S(1)}, f32[4,1,8,512]{3,2,1,0:T(8,128)S(1)}, s32[]{:T(128)}, ...), condition=%wide.region_6.7_spmd.clone, body=%wide.region_4.6_spmd.clone.sunk | while | flops 3276803 | bytes 2195543 | solution.py:65
  175.9 0.5 select_reduce_fusion.7
  176.4 0.2 bitcast_add_fusion.6
  176.6 0.5 select_reduce_fusion.7
  177.2 0.2 bitcast_add_fusion.6
  177.4 0.5 select_reduce_fusion.7
  177.9 0.2 bitcast_add_fusion.6
  178.2 0.5 select_reduce_fusion.7
  178.7 0.2 bitcast_add_fusion.6
  178.9 0.0 copy-done.2
  178.9 3.4 %fusion.6 = f32[1,256,512]{2,1,0:T(8,128)} fusion(f32[1,256,512]{2,1,0:T(8,128)S(1)} %get-tuple-element.85, bf16[256,512]{1,0:T(8,128)(2,1)S(1)} %copy-done.2, f32[1,256,512]{2,1,0:T(8,128)} %param.14, f32[256]{0:T(256)S(1)} %get-tuple-element.184, f32[256]{0:T(256)S(1)} %get-tuple-element.183), kind=kOutput, calls=%fused_computation.22 | convolution fusion | flops 403374080 | bytes 1837056 | tf_op jit(solution)/shard_map/kn,bkc->bnc/dot_general | solution.py:27
  182.4 84.1 %all-gather.5.cloned.1.call-done = bf16[32,1,32,512]{3,2,1,0:T(8,128)(2,1)} async-done(((bf16[1,1,32,512]{3,2,1,0:T(8,128)(2,1)}), bf16[32,1,32,512]{3,2,1,0:T(8,128)(2,1)}) %all-gather.5.cloned.1.call-update) | async-done | bytes 1048592 | tf_op jit(solution)/shard_map/all_gather | solution.py:97
  266.5 1.4 convert_reduce_fusion
  267.9 3.1 %while.35 = (s32[]{:T(128)}, f32[1,256,512]{2,1,0:T(8,128)S(1)}, s32[4,1,8,512]{3,2,1,0:T(8,128)S(1)}, f32[4,1,8,512]{3,2,1,0:T(8,128)S(1)}, s32[]{:T(128)}, /*index=5*/s32[]{:T(128)}) while((s32[]{:T(128)}, f32[1,256,512]{2,1,0:T(8,128)S(1)}, s32[4,1,8,512]{3,2,1,0:T(8,128)S(1)}, f32[4,1,8,512]{3,2,1,0:T(8,128)S(1)}, ...), condition=%wide.region_10.11_spmd.clone, body=%wide.region_8.10_spmd.clone.sunk | while | flops 3276803 | bytes 2195543 | solution.py:65
  267.9 0.5 select_reduce_fusion.8
  268.4 0.2 bitcast_add_fusion.7
  268.7 0.5 select_reduce_fusion.8
  269.2 0.2 bitcast_add_fusion.7
  269.5 0.5 select_reduce_fusion.8
  270.0 0.2 bitcast_add_fusion.7
  270.2 0.5 select_reduce_fusion.8
  270.8 0.2 bitcast_add_fusion.7
  271.0 1.8 fusion.7
  272.8 0.8 copy.19
  (32 shorter events, 0.2 us)
Async XLA Ops:
  7.2 1.4 copy-start
  7.2 78.8 %all-gather.3.cloned.1.call-start = ((), (), s32[]{:S(2)}) async-start(), calls=%async_computation.1 | async-start | bytes 4456448 | tf_op jit(solution)/shard_map/all_gather | solution.py:78
  7.9 160.3 %reduce-scatter.2.cloned.1.call-start = ((), (), s32[]{:S(2)}) async-start(), calls=%async_computation.2 | async-start | bytes 4456448 | tf_op jit(solution)/shard_map/reduce_scatter | solution.py:80
  12.8 73.3 %copy-start.4 = (bf16[192,512]{1,0:T(8,128)(2,1)S(1)}, bf16[192,512]{1,0:T(8,128)(2,1)}, u32[]{:S(2)}) copy-start(bf16[192,512]{1,0:T(8,128)(2,1)} %param.12) | copy-start | bytes 589828
  12.8 155.4 %copy-start.1 = (f32[1,256,512]{2,1,0:T(8,128)S(1)}, f32[1,256,512]{2,1,0:T(8,128)}, u32[]{:S(2)}) copy-start(f32[1,256,512]{2,1,0:T(8,128)} %param.14) | copy-start | bytes 1572868
  12.8 160.3 %copy-start.3 = (s32[1,32,512]{2,1,0:T(8,128)S(1)}, s32[1,32,512]{2,1,0:T(8,128)}, u32[]{:S(2)}) copy-start(s32[1,32,512]{2,1,0:T(8,128)} %param.15) | copy-start | bytes 196612
  12.8 253.6 %all-gather.5.cloned.1.call-start = ((), (), s32[]{:S(2)}) async-start(), calls=%async_computation.3 | async-start | bytes 1081344 | tf_op jit(solution)/shard_map/all_gather | solution.py:97
  175.8 3.1 %copy-start.2 = (bf16[256,512]{1,0:T(8,128)(2,1)S(1)}, bf16[256,512]{1,0:T(8,128)(2,1)}, u32[]{:S(2)}) copy-start(bf16[256,512]{1,0:T(8,128)(2,1)} %reduce-scatter.2.cloned.1.call-done) | copy-start | bytes 786436
Sparse Core Ops, SparseCore 0:
  10.1 75.8 all-gather.2
  88.9 79.2 reduce-scatter.1
  175.9 90.4 all-gather.4
where the time goes:
time: 281 us; the launch traced here: 280 us
  waiting for transfers between devices  235 us (84%)
  matrix products  17.9 us (6%)
  between operations  13.9 us (5%)
  other arithmetic  9.54 us (3%)
  local copies, waits for them, and re-layouts  2.94 us (1%)
    all_gather x1, waiting for transfers between devices, on_device(): lax.all_gather(bands[None], 'dp', axis=0, tiled=True).astype(jnp.float32)  84.1 us
    reduce_scatter x1, waiting for transfers between devices, on_device(): lax.psum_scatter(lax.dot_general(activations, cotangent, (((0,), (0,)), (...  77.3 us
    all_gather x1, waiting for transfers between devices, on_device(): lax.all_gather(weight, 'fsdp', axis=0, tiled=True)  73.1 us
  transfers between devices with their start and end apart: 3, of which 3 were waited for; matrix products, arithmetic and copies ran while one was open for 5% of the time, Pallas kernels for 0%

commit v1 on v0

v1 whole, which is shorter than its diff:
```python
import functools

import jax
import jax.numpy as jnp
import numpy as np
from jax import lax
from jax.experimental import pallas as pl
from jax.experimental.pallas import tpu as pltpu
from jax.sharding import PartitionSpec as P

NZ, NQ, NX, NY = 8, 4, 2, 8
SPAN, KV, TOPK, TOK, FEAT = 256, 512, 32, 192, 4096
HALF = FEAT // NX
SUBS = 4
MOMENTUM_DECAY = 0.999
MESH = pl.DeviceIdType.MESH
F32, BF16 = jnp.float32, jnp.bfloat16


def transform_table(length):
    freq = np.arange(length, dtype=np.float64)[:, None]
    place = np.arange(length, dtype=np.float64)[None, :]
    scales = np.where(freq == 0, np.sqrt(1.0 / length), np.sqrt(2.0 / length))
    return (scales * np.cos(np.pi * (2 * place + 1) * freq / (2 * length))).astype(np.float32)


def remote(src, dst, send, recv, dp, fsdp):
    return pltpu.make_async_remote_copy(
        src_ref=src, dst_ref=dst, send_sem=send, recv_sem=recv,
        device_id=(dp, fsdp), device_id_type=MESH,
    )


def meet(peers):
    barrier = pltpu.get_barrier_semaphore()
    for peer in peers:
        pl.semaphore_signal(barrier, inc=1, device_id=peer, device_id_type=MESH)
    pl.semaphore_wait(barrier, len(peers))


def exchange_kernel(
    a, c, w, pos, grad, full, inv,
    ax, cx, part, sbuf, rbuf, xs, xr, ys, yr, ws, wr, zs, zr, cs, cr, ls,
):
    d, f = lax.axis_index("dp"), lax.axis_index("fsdp")
    x, y = f // NY, lax.rem(f, NY)
    z, q = d // NQ, lax.rem(d, NQ)
    core = lax.rem(d, 2)
    piece = z * 2 + core
    other_x = lax.rem(f + NY, NX * NY)
    other_core = d + 1 - 2 * core

    def at_y(step):
        return x * NY + lax.rem(y + step + NY, NY)

    def at_z(step):
        return lax.rem(z + step + NZ, NZ) * NQ + q

    meet(
        [(d, other_x), (other_core, f), (at_z(1), f), (at_z(-1), f)]
        + [(d, at_y(o)) for o in range(1, NY)]
    )

    def cot_copy():
        return remote(c, cx, xs.at[8], xr.at[8], d, other_x)

    def act_copy(block):
        columns = pl.ds(pl.multiple_of((1 - x) * HALF + block * SPAN, SPAN), SPAN)
        return remote(a.at[:, columns], ax.at[block], xs.at[block], xr.at[block], d, other_x)

    def blocks_of(step):
        return lax.rem(y - 1 - step + 2 * NY, NY), lax.rem(y + 1 + step, NY)

    def own_piece(o):
        target = other_x if o == 0 else at_y(o)
        recv = wr.at[1, 0] if o == 0 else wr.at[0, o]
        return remote(w.at[piece], full.at[f, piece], ws.at[0, o], recv, d, target)

    def passed_piece(o):
        return remote(full.at[other_x, piece], full.at[other_x, piece], ws.at[1, o], wr.at[1, o], d, at_y(o))

    cot_copy().start()
    own_piece(0).start()
    for o in (4, 3, 5, 2, 6, 1, 7):
        own_piece(o).start()
    mine = pltpu.make_async_copy(w.at[piece], full.at[f, piece], ls)
    mine.start()
    for s in range(3):
        for block in blocks_of(s):
            act_copy(block).start()
    act_copy(lax.rem(y + 4, NY)).start()
    act_copy(y).start()

    @pl.loop(0, SPAN // 32)
    def _(r):
        rows = pl.ds(pl.multiple_of(r * 32, 32), 32)
        level = lax.broadcasted_iota(jnp.int32, (32, KV), 0) + r * 32
        total = jnp.full((32, KV), -1, jnp.int32)
        for i in range(TOPK):
            row = jnp.broadcast_to(pos[i : i + 1, :], (32, KV))
            total = jnp.where(row == level, i, total)
        inv[rows, :] = total

    def from_x():
        return remote(w.at[piece], full.at[other_x, piece], ws.at[0, 0], wr.at[1, 0], d, other_x)

    from_x().wait_recv()
    for o in (4, 3, 5, 2, 6, 1, 7):
        passed_piece(o).start()

    def piece_at(direction, step, which):
        at = lax.rem(z - step + NZ, NZ) if direction == 0 else lax.rem(z + step, NZ)
        return at * 2 + which

    def z_copy(direction, step, sub):
        shards = pl.ds(direction * 8 + sub * 4, 4)
        ref = full.at[shards, piece_at(direction, step, core)]
        return remote(
            ref, ref, zs.at[direction, step, sub], zr.at[direction, step, sub],
            at_z(1 if direction == 0 else -1), f,
        )

    def z_arrived(direction, step, sub):
        shards = pl.ds(direction * 8 + sub * 4, 4)
        ref = full.at[shards, piece_at(direction, step + 1, core)]
        return remote(
            ref, ref, zs.at[direction, step, sub], zr.at[direction, step, sub],
            at_z(1 if direction == 0 else -1), f,
        )

    def core_copy(direction, step):
        ref = full.at[pl.ds(direction * 8, 8), piece_at(direction, step, core)]
        return remote(ref, ref, cs.at[direction, step], cr.at[direction, step], other_core, f)

    def core_arrived(direction, step):
        ref = full.at[pl.ds(direction * 8, 8), piece_at(direction, step, 1 - core)]
        return remote(ref, ref, cs.at[direction, step], cr.at[direction, step], other_core, f)

    mine.wait()
    for o in range(1, NY):
        own = full.at[at_y(-o), piece]
        remote(own, own, ws.at[0, o], wr.at[0, o], d, at_y(o)).wait_recv()
        passed = full.at[lax.rem(at_y(-o) + NY, NX * NY), piece]
        remote(passed, passed, ws.at[1, o], wr.at[1, o], d, at_y(o)).wait_recv()
    for direction in range(2):
        for sub in range(2):
            z_copy(direction, 0, sub).start()
    for direction in range(2):
        core_copy(direction, 0).start()

    def product(block):
        act_copy(block).wait_recv()
        own = a[:, pl.ds(pl.multiple_of(x * HALF + block * SPAN, SPAN), SPAN)]
        dims = (((0,), (0,)), ((), ()))
        part[block] = lax.dot_general(own, c[...], dims, preferred_element_type=F32) + lax.dot_general(
            ax[block], cx[...], dims, preferred_element_type=F32
        )

    rows_of = SPAN // SUBS

    def y_copy(direction, step, sub):
        rows = pl.ds(sub * rows_of, rows_of)
        return remote(
            sbuf.at[direction, step, rows], rbuf.at[direction, step, rows],
            ys.at[direction, step, sub], yr.at[direction, step, sub],
            d, at_y(1 if direction == 0 else -1),
        )

    def y_send(step, first):
        blocks = blocks_of(step)
        for sub in range(SUBS):
            for direction in range(2):
                rows = pl.ds(sub * rows_of, rows_of)
                columns = pl.ds(direction * SPAN, SPAN)
                value = part[blocks[direction], rows, columns]
                if not first:
                    y_copy(direction, step - 1, sub).wait_recv()
                    value = value + rbuf[direction, step - 1, rows].astype(F32)
                sbuf[direction, step, rows] = value.astype(BF16)
                y_copy(direction, step, sub).start()

    cot_copy().wait_recv()
    for block in blocks_of(0):
        product(block)
    y_send(0, True)

    @pl.loop(1, 7)
    def _(step):
        back, ahead = blocks_of(step)

        @pl.when(step < 4)
        def _():
            product(back)

        @pl.when(step < 3)
        def _():
            product(ahead)

        @pl.when(step == 4)
        def _():
            product(y)

        y_send(step, False)
        for direction in range(2):
            for sub in range(2):
                z_arrived(direction, step - 1, sub).wait_recv()
                z_copy(direction, step, sub).start()
            core_copy(direction, step).start()

    for sub in range(SUBS):
        for direction in range(2):
            rows = pl.ds(sub * rows_of, rows_of)
            columns = pl.ds(direction * SPAN, SPAN)
            y_copy(direction, 6, sub).wait_recv()
            grad[rows, columns] = part[y, rows, columns] + rbuf[direction, 6, rows].astype(F32)
    for direction in range(2):
        for sub in range(2):
            z_arrived(direction, 6, sub).wait_recv()
        core_copy(direction, 7).start()

    cot_copy().wait_send()
    for o in range(NY):
        own_piece(o).wait_send()
    for o in range(1, NY):
        passed_piece(o).wait_send()

    @pl.loop(0, 8)
    def _(step):
        act_copy(step).wait_send()
        for direction in range(2):
            core_copy(direction, step).wait_send()
            core_arrived(direction, step).wait_recv()

    @pl.loop(0, 7)
    def _(step):
        for direction in range(2):
            for sub in range(SUBS):
                y_copy(direction, step, sub).wait_send()
            for sub in range(2):
                z_copy(direction, step, sub).wait_send()


def exchange(activations, cotangent, weight, positions):
    vmem = pl.BlockSpec(memory_space=pltpu.VMEM)
    dma = pltpu.SemaphoreType.DMA
    return pl.pallas_call(
        exchange_kernel,
        out_shape=(
            jax.ShapeDtypeStruct((SPAN, KV), F32),
            jax.ShapeDtypeStruct((16, 16, 16, KV), BF16),
            jax.ShapeDtypeStruct((SPAN, KV), jnp.int32),
        ),
        in_specs=[vmem] * 4,
        out_specs=(vmem, pl.BlockSpec(memory_space=pl.ANY), vmem),
        scratch_shapes=[
            pltpu.VMEM((NY, TOK, SPAN), BF16),
            pltpu.VMEM((TOK, KV), BF16),
            pltpu.VMEM((NY, SPAN, KV), F32),
            pltpu.VMEM((2, 7, SPAN, SPAN), BF16),
            pltpu.VMEM((2, 7, SPAN, SPAN), BF16),
            dma((9,)), dma((9,)),
            dma((2, 7, SUBS)), dma((2, 7, SUBS)),
            dma((2, NY)), dma((2, NY)),
            dma((2, 7, 2)), dma((2, 7, 2)),
            dma((2, 8)), dma((2, 8)),
            dma,
        ],
        compiler_params=pltpu.CompilerParams(
            collective_id=0, has_side_effects=True, vmem_limit_bytes=32 << 20
        ),
        name="exchange",
    )(activations, cotangent, weight.reshape(16, 16, KV), positions)


def pick_rows(values, where, groups):
    low, high = where & 7, where >> 3
    found = jnp.zeros(where.shape, values.dtype)
    for group in range(groups):
        rows = jnp.take_along_axis(values[group * 8 : group * 8 + 8, :], low, axis=0)
        found = jnp.where(high == group, rows, found)
    return found


def dot_full(left, right, dims):
    return lax.dot_general(
        left, right, (dims, ((), ())), precision=lax.Precision.HIGHEST, preferred_element_type=F32
    )


def momentum_kernel(table, grad, momentum, pos, inv, kept, bands, coeffs):
    moment = MOMENTUM_DECAY * momentum[0] + grad[...]
    found = dot_full(table[...], moment, ((1,), (0,)))
    coeffs[...] = found
    masked = jnp.where(inv[...] >= 0, found, 0.0)
    for column in range(KV // 128):
        lanes = pl.ds(column * 128, 128)
        picked = [
            pick_rows(coeffs[:, lanes], pos[pl.ds(r * 8, 8), lanes], SPAN // 8) for r in range(TOPK // 8)
        ]
        bands[:, lanes] = jnp.concatenate(picked, axis=0).astype(BF16)
    kept[0] = moment - dot_full(table[...], masked, ((0,), (0,)))


def step_momentum(table, grad, momentum, positions, inv):
    vmem = pl.BlockSpec(memory_space=pltpu.VMEM)
    return pl.pallas_call(
        momentum_kernel,
        out_shape=(
            jax.ShapeDtypeStruct((1, SPAN, KV), F32),
            jax.ShapeDtypeStruct((TOPK, KV), BF16),
        ),
        in_specs=[vmem] * 5,
        out_specs=(vmem, vmem),
        scratch_shapes=[pltpu.VMEM((SPAN, KV), F32)],
        name="momentum",
    )(table, grad, momentum, positions, inv)


def bands_kernel(bands, c, full, mean, out, first, second, total, third, ss, sr):
    d, f = lax.axis_index("dp"), lax.axis_index("fsdp")
    z, q = d // NQ, lax.rem(d, NQ)
    hi, core = q // 2, lax.rem(q, 2)

    def at_q(k):
        flip_hi, flip_core = k // 2, k % 2
        new_hi = 1 - hi if flip_hi else hi
        new_core = 1 - core if flip_core else core
        return new_hi * 2 + new_core

    def at_z(step):
        return lax.rem(z + step + NZ, NZ)

    meet([(z * NQ + at_q(k), f) for k in range(1, 4)] + [(at_z(o) * NQ + q, f) for o in range(1, NZ)])

    def one(k):
        columns = pl.ds(pl.multiple_of(at_q(k) * 128, 128), 128)
        return remote(bands.at[:, columns], first.at[k - 1], ss.at[0, k], sr.at[0, k], z * NQ + at_q(k), f)

    def two(o):
        return remote(total, second.at[z], ss.at[1, o], sr.at[1, o], at_z(o) * NQ + q, f)

    def two_arrived(o):
        return remote(total, second.at[at_z(-o)], ss.at[1, o], sr.at[1, o], at_z(o) * NQ + q, f)

    def three(k):
        return remote(third.at[q], third.at[q], ss.at[2, k], sr.at[2, k], z * NQ + at_q(k), f)

    def three_arrived(k):
        slot = third.at[at_q(k)]
        return remote(slot, slot, ss.at[2, k], sr.at[2, k], z * NQ + at_q(k), f)

    def products(low, high):
        @pl.loop(low, high)
        def _(tile):
            rows = pl.ds(pl.multiple_of(tile * 512, 512), 512)
            out[:, rows] = lax.dot_general(
                c[...], full[rows, :], (((1,), (1,)), ((), ())), preferred_element_type=F32
            ).astype(BF16)

    for k in (3, 2, 1):
        one(k).start()
    products(0, 2)
    summed = bands[:, pl.ds(pl.multiple_of(q * 128, 128), 128)].astype(F32)
    for k in (1, 2, 3):
        one(k).wait_recv()
        summed = summed + first[k - 1].astype(F32)
    total[...] = summed
    for o in (4, 3, 5, 2, 6, 1, 7):
        two(o).start()
    second[z] = summed
    products(2, 6)
    for o in range(1, NZ):
        two_arrived(o).wait_recv()
    summed = second[0]
    for at in range(1, NZ):
        summed = summed + second[at]
    third[q] = summed / 32.0
    for k in (3, 2, 1):
        three(k).start()
    products(6, 8)
    for k in (1, 2, 3):
        three_arrived(k).wait_recv()
    for at in range(NQ):
        mean[:, at * 128 : at * 128 + 128] = third[at]
    for k in (1, 2, 3):
        one(k).wait_send()
        three(k).wait_send()
    for o in range(1, NZ):
        two(o).wait_send()


def reduce_bands(bands, cotangent, full):
    vmem = pl.BlockSpec(memory_space=pltpu.VMEM)
    dma = pltpu.SemaphoreType.DMA
    return pl.pallas_call(
        bands_kernel,
        out_shape=(
            jax.ShapeDtypeStruct((TOPK, KV), F32),
            jax.ShapeDtypeStruct((TOK, FEAT), BF16),
        ),
        in_specs=[vmem] * 3,
        out_specs=(vmem, vmem),
        scratch_shapes=[
            pltpu.VMEM((3, TOPK, 128), BF16),
            pltpu.VMEM((NZ, TOPK, 128), F32),
            pltpu.VMEM((TOPK, 128), F32),
            pltpu.VMEM((NQ, TOPK, 128), F32),
            dma((3, 8)), dma((3, 8)),
        ],
        compiler_params=pltpu.CompilerParams(
            collective_id=1, has_side_effects=True, vmem_limit_bytes=32 << 20
        ),
        name="bands",
    )(bands, cotangent, full)


def update_kernel(table, mean, inv, given, update, result, dense, sem):
    copy = pltpu.make_async_copy(given, result, sem)
    copy.start()
    for column in range(KV // 128):
        lanes = pl.ds(column * 128, 128)
        for r in range(SPAN // 8):
            dense[pl.ds(r * 8, 8), lanes] = pick_rows(mean[:, lanes], inv[pl.ds(r * 8, 8), lanes], TOPK // 8)
    update[...] = dot_full(table[...], dense[...], ((0,), (0,))).astype(BF16)
    copy.wait()


def decode(table, mean, inv, given):
    vmem = pl.BlockSpec(memory_space=pltpu.VMEM)
    return pl.pallas_call(
        update_kernel,
        out_shape=(
            jax.ShapeDtypeStruct((SPAN, KV), BF16),
            jax.ShapeDtypeStruct((TOK, FEAT), BF16),
        ),
        in_specs=[vmem] * 4,
        out_specs=(vmem, pl.BlockSpec(memory_space=pl.ANY)),
        scratch_shapes=[pltpu.VMEM((SPAN, KV), F32), pltpu.SemaphoreType.DMA],
        name="decode",
    )(table, mean, inv, given)


def on_device(activations, cotangent, weight, momentum, positions):
    table = jnp.asarray(transform_table(SPAN))
    where = positions[0]
    grad, full, inv = exchange(activations, cotangent, weight, where)
    kept, bands = step_momentum(table, grad, momentum, where, inv)
    mean, product = reduce_bands(bands, cotangent, full.reshape(FEAT, KV))
    update, grad_input = decode(table, mean, inv, product)
    return grad_input, kept, update


def solution(mesh):
    placed = (
        P(("dp", "fsdp"), None),
        P(("dp", "fsdp"), None),
        P("fsdp", None),
        P("dp", "fsdp", None),
        P("fsdp", None, None),
    )
    return jax.shard_map(
        on_device,
        mesh=mesh,
        in_specs=placed,
        out_specs=(P(("dp", "fsdp"), None), P("dp", "fsdp", None), P("fsdp", None)),
        check_vma=False,
    )
```

time: 281 us -> 98.3 us (0.35)
  waiting for transfers between devices: 235 us -> 0 us
  Pallas kernels: 0 us -> 84.8 us
  matrix products: 17.9 us -> 0 us
  between operations: 13.9 us -> 0.68 us
  other arithmetic: 9.54 us -> 0 us
  local copies, waits for them, and re-layouts: 2.94 us -> 12.4 us
    all_gather x2 -> x0, waiting for transfers between devices: 157 us -> none  [the longest x1 84.1 us: on_device(): lax.all_gather(bands[None], 'dp', axis=0, tiled=True).astype(jnp.float32)]
    pallas_call x0 -> x4, Pallas kernels: none -> 84.8 us  [the longest x1 61.6 us: exchange(): pl.pallas_call(exchange_kernel, out_shape=(jax.ShapeDtypeStruct((SPAN, KV...]
    reduce_scatter x1 -> x0, waiting for transfers between devices: 77.3 us -> none  [on_device(): lax.psum_scatter(lax.dot_general(activations, cotangent, (((0,), (0,)), (...]
    dot_general x5 -> x0, matrix products: 17.9 us -> none  [the longest x2 5.26 us: inverse_blocks(): jnp.einsum('kn,bkc->bnc', table, coeffs, precision=lax.Precision.HIGHEST)]
    unnamed x12 -> x24, local copies, waits for them, and re-layouts: 2.72 us -> 12.4 us
    reduce_sum x13 -> x0, other arithmetic: 7.45 us -> none  [the longest x8 4.22 us: add_group(): jnp.sum(jnp.where(onehot, amounts[:, :, None, :], 0.0), axis=1)]
  transfers between devices with their start and end apart: 3 -> 0, of which waited for: 3 -> 0; matrix products, arithmetic and copies ran while one was open for 5% -> 0% of each run, Pallas kernels for 0% -> 0%
where the time goes in v1:
time: 98.3 us; the launch traced here: 97.9 us
  Pallas kernels  84.8 us (86%)
  local copies, waits for them, and re-layouts  12.4 us (13%)
    pallas_call x1, Pallas kernels, exchange(): pl.pallas_call(exchange_kernel, out_shape=(jax.ShapeDtypeStruct((SPAN, KV...  61.6 us
    pallas_call x1, Pallas kernels, reduce_bands(): pl.pallas_call(bands_kernel, out_shape=(jax.ShapeDtypeStruct((TOPK, KV),...  15.9 us
    unnamed x24, local copies, waits for them, and re-layouts  12.4 us
    pallas_call x1, Pallas kernels, step_momentum(): pl.pallas_call(momentum_kernel, out_shape=(jax.ShapeDtypeStruct((1, SPAN,...  3.7 us
    pallas_call x1, Pallas kernels, decode(): pl.pallas_call(update_kernel, out_shape=(jax.ShapeDtypeStruct((SPAN, KV),...  3.54 us

profile of v1, /device:TPU:1, one launch (start us, length us, event | category | flops | bytes accessed | tf_op | source)
XLA Modules:
  0.0 97.9 jit_solution(6613287682471358963)
XLA Ops:
  0.6 0.0 copy-start.4
  0.6 1.4 %copy-done.4 = bf16[192,4096]{1,0:T(8,128)(2,1)S(1)} copy-done((bf16[192,4096]{1,0:T(8,128)(2,1)S(1)}, bf16[192,4096]{1,0:T(8,128)(2,1)}, u32[]{:S(2)}) %copy-start.4) | copy-done | bytes 1572888
  2.0 0.0 copy-start.5
  2.0 0.9 copy-done.5
  3.0 0.0 copy-start.8
  3.0 0.9 copy-done.8
  3.9 0.0 copy-start.9
  3.9 0.8 copy-done.9
  4.8 0.0 copy-start.6
  4.8 61.6 %exchange.1 = (f32[256,512]{1,0:T(8,128)S(1)}, bf16[16,16,16,512]{3,2,1,0:T(8,128)(2,1)S(1)}, s32[256,512]{1,0:T(8,128)S(1)}) custom-call(bf16[192,4096]{1,0:T(8,128)(2,1)S(1)} %copy-done.4, bf16[192,512]{1,0:T(8,128)(2,1)S(1)} %copy-done.5, bf16[16,16,512]{2,1,0:T(8,128)(2,1)S(1)} %bitcast.4, s32[32,512]{1,0:T(8,128)S(1)} %bitcast.6), custom_call_target="tpu_custom_call" | custom-call | tf_op jit(solution)/shard_map/exchange/pallas_call | solution.py:246
  66.4 0.0 copy-start
  66.4 1.9 %copy-done = bf16[16,16,16,512]{3,2,1,0:T(8,128)(2,1)} copy-done((bf16[16,16,16,512]{3,2,1,0:T(8,128)(2,1)}, bf16[16,16,16,512]{3,2,1,0:T(8,128)(2,1)S(1)}, u32[]{:S(2)}) %copy-start) | copy-done | bytes 4194328
  68.3 0.0 copy-start.2
  68.3 0.8 copy-done.2
  69.1 0.0 copy-start.7
  69.1 0.8 copy-done.7
  69.9 3.7 %momentum.2 = (f32[1,256,512]{2,1,0:T(8,128)}, bf16[32,512]{1,0:T(8,128)(2,1)}) custom-call(f32[256,256]{1,0:T(8,128)} %constant.2.clone.table, f32[256,512]{1,0:T(8,128)} %copy-done.7, f32[1,256,512]{2,1,0:T(8,128)} %momentum.3, s32[32,512]{1,0:T(8,128)} %bitcast.5, s32[256,512]{1,0:T(8,128)} %copy-done.2), custom_call_target="tpu_custom_call" | custom-call | tf_op jit(solution)/shard_map/momentum/pallas_call | solution.py:306
  73.6 0.0 copy-done.6
  73.6 0.0 copy-start.1
  73.6 2.2 %copy-done.1 = bf16[16,16,16,512]{3,2,1,0:T(8,128)(2,1)S(1)} copy-done((bf16[16,16,16,512]{3,2,1,0:T(8,128)(2,1)S(1)}, bf16[16,16,16,512]{3,2,1,0:T(8,128)(2,1)}, u32[]{:S(2)}) %copy-start.1) | copy-done | bytes 4194328
  75.8 0.0 copy-start.11
  75.8 0.8 copy-done.11
  76.6 15.9 %bands.1 = (f32[32,512]{1,0:T(8,128)S(1)}, bf16[192,4096]{1,0:T(8,128)(2,1)S(1)}) custom-call(bf16[32,512]{1,0:T(8,128)(2,1)S(1)} %copy-done.11, bf16[192,512]{1,0:T(8,128)(2,1)S(1)} %copy-done.6, bf16[4096,512]{1,0:T(8,128)(2,1)S(1)} %bitcast.3), custom_call_target="tpu_custom_call" | custom-call | tf_op jit(solution)/shard_map/bands/pallas_call | solution.py:395
  92.5 0.0 copy-start.3
  92.5 1.2 %copy-done.3 = bf16[192,4096]{1,0:T(8,128)(2,1)} copy-done((bf16[192,4096]{1,0:T(8,128)(2,1)}, bf16[192,4096]{1,0:T(8,128)(2,1)S(1)}, u32[]{:S(2)}) %copy-start.3) | copy-done | bytes 1572888
  93.7 0.0 copy-start.10
  93.7 0.6 copy-done.10
  94.3 3.5 %decode.1 = (bf16[256,512]{1,0:T(8,128)(2,1)}, bf16[192,4096]{1,0:T(8,128)(2,1)}) custom-call(f32[256,256]{1,0:T(8,128)} %constant.2.clone.table, f32[32,512]{1,0:T(8,128)} %copy-done.10, s32[256,512]{1,0:T(8,128)} %copy-done.2, bf16[192,4096]{1,0:T(8,128)(2,1)} %copy-done.3), custom_call_target="tpu_custom_call" | custom-call | tf_op jit(solution)/shard_map/decode/pallas_call | solution.py:430
Async XLA Ops:
  0.6 1.4 %copy-start.4 = (bf16[192,4096]{1,0:T(8,128)(2,1)S(1)}, bf16[192,4096]{1,0:T(8,128)(2,1)}, u32[]{:S(2)}) copy-start(bf16[192,4096]{1,0:T(8,128)(2,1)} %a.1) | copy-start | bytes 4718596
  2.0 0.9 copy-start.5
  3.0 0.9 copy-start.8
  3.9 0.8 copy-start.9
  4.8 68.9 %copy-start.6 = (bf16[192,512]{1,0:T(8,128)(2,1)S(1)}, bf16[192,512]{1,0:T(8,128)(2,1)}, u32[]{:S(2)}) copy-start(bf16[192,512]{1,0:T(8,128)(2,1)} %c.3) | copy-start | bytes 589828
  66.4 2.0 %copy-start = (bf16[16,16,16,512]{3,2,1,0:T(8,128)(2,1)}, bf16[16,16,16,512]{3,2,1,0:T(8,128)(2,1)S(1)}, u32[]{:S(2)}) copy-start(bf16[16,16,16,512]{3,2,1,0:T(8,128)(2,1)S(1)} %get-tuple-element.15) | copy-start | bytes 12582916
  68.3 0.8 copy-start.2
  69.1 0.8 copy-start.7
  73.6 2.2 %copy-start.1 = (bf16[16,16,16,512]{3,2,1,0:T(8,128)(2,1)S(1)}, bf16[16,16,16,512]{3,2,1,0:T(8,128)(2,1)}, u32[]{:S(2)}) copy-start(bf16[16,16,16,512]{3,2,1,0:T(8,128)(2,1)} %copy-done) | copy-start | bytes 12582916
  75.8 0.8 copy-start.11
  92.5 1.2 %copy-start.3 = (bf16[192,4096]{1,0:T(8,128)(2,1)}, bf16[192,4096]{1,0:T(8,128)(2,1)S(1)}, u32[]{:S(2)}) copy-start(bf16[192,4096]{1,0:T(8,128)(2,1)S(1)} %get-tuple-element.17.given) | copy-start | bytes 4718596
  93.7 0.6 copy-start.10

commit v2 on v0

v2 whole, which is shorter than its diff:
```python
import functools

import jax
import jax.numpy as jnp
import numpy as np
from jax import lax
from jax.experimental import pallas as pl
from jax.experimental.pallas import tpu as pltpu
from jax.sharding import PartitionSpec as P

NZ, NQ, NX, NY = 8, 4, 2, 8
SPAN, KV, TOPK, TOK, FEAT = 256, 512, 32, 192, 4096
HALF = FEAT // NX
SUBS = 4
TOKENS_IN = (((0,), (0,)), ((), ()))
MOMENTUM_DECAY = 0.999
MESH = pl.DeviceIdType.MESH
F32, BF16 = jnp.float32, jnp.bfloat16


def transform_table(length):
    freq = np.arange(length, dtype=np.float64)[:, None]
    place = np.arange(length, dtype=np.float64)[None, :]
    scales = np.where(freq == 0, np.sqrt(1.0 / length), np.sqrt(2.0 / length))
    return (scales * np.cos(np.pi * (2 * place + 1) * freq / (2 * length))).astype(np.float32)


def remote(src, dst, send, recv, dp, fsdp):
    return pltpu.make_async_remote_copy(
        src_ref=src, dst_ref=dst, send_sem=send, recv_sem=recv,
        device_id=(dp, fsdp), device_id_type=MESH,
    )


def meet(peers):
    barrier = pltpu.get_barrier_semaphore()
    for peer in peers:
        pl.semaphore_signal(barrier, inc=1, device_id=peer, device_id_type=MESH)
    pl.semaphore_wait(barrier, len(peers))


def pick_rows(values, where, groups):
    low, high = where & 7, where >> 3
    found = jnp.zeros(where.shape, values.dtype)
    for group in range(groups):
        rows = jnp.take_along_axis(values[group * 8 : group * 8 + 8, :], low, axis=0)
        found = jnp.where(high == group, rows, found)
    return found


def dot_full(left, right, dims):
    return lax.dot_general(
        left, right, (dims, ((), ())), precision=lax.Precision.HIGHEST, preferred_element_type=F32
    )


def step_kernel(
    a, c, w, momentum, positions, table,
    kept, out, mean, inv,
    av, cv, pos, tv, mv, ax, cx, part, full, half_s, half_r, block_s, block_r,
    coeffs, bands, first, total, second, third,
    ls, xs, xr, hs, hr, ys, yr, ws, wr, zs, zr, cs, cr, ss, sr,
):
    d, f = lax.axis_index("dp"), lax.axis_index("fsdp")
    x, y = f // NY, lax.rem(f, NY)
    z, q = d // NQ, lax.rem(d, NQ)
    hi, core = q // 2, lax.rem(q, 2)
    piece = z * 2 + core
    other_x = lax.rem(f + NY, NX * NY)
    other_core = d + 1 - 2 * core

    def wrap_y(at):
        return lax.rem(at + 2 * NY, NY)

    def wrap_z(at):
        return lax.rem(at + 2 * NZ, NZ)

    def at_y(step):
        return x * NY + wrap_y(y + step)

    def at_z(step):
        return wrap_z(z + step) * NQ + q

    def at_q(k):
        new_hi = 1 - hi if k // 2 else hi
        new_core = 1 - core if k % 2 else core
        return new_hi * 2 + new_core

    local = [
        pltpu.make_async_copy(positions, pos, ls.at[0]),
        pltpu.make_async_copy(c, cv, ls.at[1]),
        pltpu.make_async_copy(a.at[:, pl.ds(pl.multiple_of(x * HALF, HALF), HALF)], av, ls.at[2]),
        pltpu.make_async_copy(w.at[piece], full.at[f, piece], ls.at[3]),
        pltpu.make_async_copy(table, tv, ls.at[4]),
        pltpu.make_async_copy(momentum, mv, ls.at[5]),
    ]
    for copy in local:
        copy.start()

    meet(
        [(d, other_x)]
        + [(d, at_y(o)) for o in range(1, NY)]
        + [(at_z(o), f) for o in range(1, NZ)]
        + [(z * NQ + at_q(k), f) for k in range(1, NQ)]
    )

    def cot_copy():
        return remote(c, cx, xs.at[8], xr.at[8], d, other_x)

    def act_copy(block):
        columns = pl.ds(pl.multiple_of((1 - x) * HALF + block * SPAN, SPAN), SPAN)
        return remote(a.at[:, columns], ax.at[block], xs.at[block], xr.at[block], d, other_x)

    def own_piece(o):
        target = other_x if o == 0 else at_y(o)
        recv = wr.at[1, 0] if o == 0 else wr.at[0, o]
        return remote(w.at[piece], full.at[f, piece], ws.at[0, o], recv, d, target)

    def passed_piece(o):
        ref = full.at[other_x, piece]
        return remote(ref, ref, ws.at[1, o], wr.at[1, o], d, at_y(o))

    far_first = (4, 3, 5, 2, 6, 1, 7)
    own_piece(0).start()
    cot_copy().start()
    for o in far_first:
        own_piece(o).start()
    for o in (4, 3, -3, 2, -2, 1, -1, 0):
        act_copy(wrap_y(y + o)).start()

    local[0].wait()

    @pl.loop(0, SPAN // 32)
    def _(r):
        rows = pl.ds(pl.multiple_of(r * 32, 32), 32)
        level = lax.broadcasted_iota(jnp.int32, (32, KV), 0) + r * 32
        found = jnp.full((32, KV), -1, jnp.int32)
        for i in range(TOPK):
            row = jnp.broadcast_to(pos[i : i + 1, :], (32, KV))
            found = jnp.where(row == level, i, found)
        inv[rows, :] = found

    passed = full.at[other_x, piece]
    remote(w.at[piece], passed, ws.at[0, 0], wr.at[1, 0], d, other_x).wait_recv()
    for o in far_first:
        passed_piece(o).start()

    local[1].wait()
    local[2].wait()

    @pl.loop(0, NY)
    def _(block):
        columns = pl.ds(pl.multiple_of(block * SPAN, SPAN), SPAN)
        part[block] = lax.dot_general(av[:, columns], cv[...], TOKENS_IN, preferred_element_type=F32)

    def product(block):
        act_copy(block).wait_recv()
        part[block] += lax.dot_general(ax[block], cx[...], TOKENS_IN, preferred_element_type=F32)

    rows_of = SPAN // SUBS

    def half_copy(direction, sub):
        rows = pl.ds(sub * rows_of, rows_of)
        return remote(
            half_s.at[direction, rows], half_r.at[direction, rows], hs.at[direction, sub], hr.at[direction, sub],
            d, at_y(1 - 2 * direction),
        )

    def block_copy(direction, step, sub):
        rows = pl.ds(sub * rows_of, rows_of)
        return remote(
            block_s.at[direction, step, rows], block_r.at[direction, step, rows],
            ys.at[direction, step, sub], yr.at[direction, step, sub],
            d, at_y(1 - 2 * direction),
        )

    def send_halves():
        block = wrap_y(y + 4)
        for sub in range(SUBS):
            for direction in range(2):
                rows, columns = pl.ds(sub * rows_of, rows_of), pl.ds(direction * SPAN, SPAN)
                half_s[direction, rows] = part[block, rows, columns].astype(BF16)
                half_copy(direction, sub).start()

    def send_blocks(step):
        for sub in range(SUBS):
            for direction in range(2):
                rows = pl.ds(sub * rows_of, rows_of)
                block = wrap_y(y + (3 - step) * (1 - 2 * direction))
                if step == 0:
                    mine, others = pl.ds(direction * SPAN, SPAN), pl.ds((1 - direction) * SPAN, SPAN)
                    half_copy(direction, sub).wait_recv()
                    value = part[block, rows, mine] + half_r[direction, rows].astype(F32)
                    block_s[direction, step, rows, mine] = value.astype(BF16)
                    block_s[direction, step, rows, others] = part[block, rows, others].astype(BF16)
                else:
                    block_copy(direction, step - 1, sub).wait_recv()
                    value = part[block, rows, :] + block_r[direction, step - 1, rows].astype(F32)
                    block_s[direction, step, rows] = value.astype(BF16)
                block_copy(direction, step, sub).start()

    def z_block(direction, step, which):
        return wrap_z(z - step * (1 - 2 * direction)) * 2 + which

    def z_copy(direction, step, sub, arriving=0):
        ref = full.at[pl.ds(sub * 8, 8), z_block(direction, step + arriving, core)]
        return remote(
            ref, ref, zs.at[direction, step, sub], zr.at[direction, step, sub], at_z(1 - 2 * direction), f
        )

    def core_copy(direction, step, sub, which):
        ref = full.at[pl.ds(sub * 8, 8), z_block(direction, step, which)]
        return remote(ref, ref, cs.at[direction, step, sub], cr.at[direction, step, sub], other_core, f)

    def halves_of(direction, step):
        return (0, 1) if step < 3 else (direction,)

    forwards = [(0, 0, 0), (0, 0, 1)] + [
        (direction, step, sub)
        for step in range(1, 5)
        for direction in range(2)
        for sub in halves_of(direction, step - 1)
    ]

    def relay(step):
        for direction in range(2):
            for sub in halves_of(direction, step - 1):
                z_copy(direction, step - 1, sub, arriving=1).wait_recv()
                if step < 4 and sub in halves_of(direction, step):
                    z_copy(direction, step, sub).start()
                core_copy(direction, step, sub, core).start()

    cot_copy().wait_recv()
    product(wrap_y(y + 4))
    send_halves()
    for o in (3, -3):
        product(wrap_y(y + o))
    send_blocks(0)

    local[3].wait()
    for o in range(1, NY):
        ref = full.at[at_y(-o), piece]
        remote(ref, ref, ws.at[0, o], wr.at[0, o], d, at_y(o)).wait_recv()
        ref = full.at[lax.rem(at_y(-o) + NY, NX * NY), piece]
        remote(ref, ref, ws.at[1, o], wr.at[1, o], d, at_y(o)).wait_recv()
    for direction in range(2):
        for sub in range(2):
            z_copy(direction, 0, sub).start()
    for sub in range(2):
        core_copy(0, 0, sub, core).start()

    for o in (2, -2):
        product(wrap_y(y + o))
    send_blocks(1)
    relay(1)
    for o in (1, -1):
        product(wrap_y(y + o))
    send_blocks(2)
    relay(2)
    product(y)
    local[5].wait()
    for sub in range(SUBS):
        rows = pl.ds(sub * rows_of, rows_of)
        gradient = part[y, rows, :]
        for direction in range(2):
            block_copy(direction, 2, sub).wait_recv()
            gradient = gradient + block_r[direction, 2, rows].astype(F32)
        mv[rows, :] = MOMENTUM_DECAY * mv[rows, :] + gradient

    local[4].wait()
    coeffs[...] = dot_full(tv[...], mv[...], ((1,), (0,)))
    for column in range(KV // 128):
        lanes = pl.ds(column * 128, 128)
        picked = [
            pick_rows(coeffs[:, lanes], pos[pl.ds(r * 8, 8), lanes], SPAN // 8) for r in range(TOPK // 8)
        ]
        bands[:, lanes] = jnp.concatenate(picked, axis=0).astype(BF16)

    def one(k):
        columns = pl.ds(pl.multiple_of(at_q(k) * 128, 128), 128)
        return remote(bands.at[:, columns], first.at[k - 1], ss.at[0, k], sr.at[0, k], z * NQ + at_q(k), f)

    def two(o):
        return remote(total, second.at[z], ss.at[1, o], sr.at[1, o], at_z(o), f)

    def two_arrived(o):
        return remote(total, second.at[wrap_z(z - o)], ss.at[1, o], sr.at[1, o], at_z(o), f)

    def three(k):
        return remote(third.at[q], third.at[q], ss.at[2, k], sr.at[2, k], z * NQ + at_q(k), f)

    def three_arrived(k):
        slot = third.at[at_q(k)]
        return remote(slot, slot, ss.at[2, k], sr.at[2, k], z * NQ + at_q(k), f)

    def grad_inputs(low, high):
        @pl.loop(low, high)
        def _(tile):
            columns = pl.ds(pl.multiple_of(tile * 512, 512), 512)
            rows = full[pl.ds(tile * 2, 2)].reshape(512, KV)
            out[:, columns] = lax.dot_general(
                cv[...], rows, (((1,), (1,)), ((), ())), preferred_element_type=F32
            ).astype(BF16)

    for k in (3, 2, 1):
        one(k).start()
    relay(3)
    masked = jnp.where(inv[...] >= 0, coeffs[...], 0.0)
    kept[0] = mv[...] - dot_full(tv[...], masked, ((0,), (0,)))
    summed = bands[:, pl.ds(pl.multiple_of(q * 128, 128), 128)].astype(F32)
    for k in range(1, NQ):
        one(k).wait_recv()
        summed = summed + first[k - 1].astype(F32)
    total[...] = summed.astype(BF16)
    for o in far_first:
        two(o).start()
    second[z] = summed.astype(BF16)
    relay(4)
    for direction, step, sub in forwards:
        core_copy(direction, step, sub, 1 - core).wait_recv()
    grad_inputs(0, 5)
    for o in range(1, NZ):
        two_arrived(o).wait_recv()
    summed = second[0].astype(F32)
    for at in range(1, NZ):
        summed = summed + second[at].astype(F32)
    third[q] = summed / (NZ * NQ)
    for k in (3, 2, 1):
        three(k).start()
    grad_inputs(5, 8)
    for k in range(1, NQ):
        three_arrived(k).wait_recv()
    for at in range(NQ):
        mean[:, at * 128 : at * 128 + 128] = third[at]

    cot_copy().wait_send()
    for o in range(NY):
        act_copy(o).wait_send()
        own_piece(o).wait_send()
    for o in range(1, NY):
        passed_piece(o).wait_send()
    for direction in range(2):
        for sub in range(SUBS):
            half_copy(direction, sub).wait_send()
            for step in range(3):
                block_copy(direction, step, sub).wait_send()
        for step in range(4):
            for sub in halves_of(direction, step):
                z_copy(direction, step, sub).wait_send()
    for direction, step, sub in forwards:
        core_copy(direction, step, sub, core).wait_send()
    for k in range(1, NQ):
        one(k).wait_send()
        three(k).wait_send()
    for o in range(1, NZ):
        two(o).wait_send()


def step(activations, cotangent, weight, momentum, positions, table):
    hbm, vmem = pl.BlockSpec(memory_space=pltpu.HBM), pl.BlockSpec(memory_space=pltpu.VMEM)
    dma = pltpu.SemaphoreType.DMA
    return pl.pallas_call(
        step_kernel,
        out_shape=(
            jax.ShapeDtypeStruct((1, SPAN, KV), F32),
            jax.ShapeDtypeStruct((TOK, FEAT), BF16),
            jax.ShapeDtypeStruct((TOPK, KV), F32),
            jax.ShapeDtypeStruct((SPAN, KV), jnp.int32),
        ),
        in_specs=[hbm] * 6,
        out_specs=(vmem,) * 4,
        scratch_shapes=[
            pltpu.VMEM((TOK, HALF), BF16),
            pltpu.VMEM((TOK, KV), BF16),
            pltpu.VMEM((TOPK, KV), jnp.int32),
            pltpu.VMEM((SPAN, SPAN), F32),
            pltpu.VMEM((SPAN, KV), F32),
            pltpu.VMEM((NY, TOK, SPAN), BF16),
            pltpu.VMEM((TOK, KV), BF16),
            pltpu.VMEM((NY, SPAN, KV), F32),
            pltpu.VMEM((16, 16, 16, KV), BF16),
            pltpu.VMEM((2, SPAN, SPAN), BF16),
            pltpu.VMEM((2, SPAN, SPAN), BF16),
            pltpu.VMEM((2, 3, SPAN, KV), BF16),
            pltpu.VMEM((2, 3, SPAN, KV), BF16),
            pltpu.VMEM((SPAN, KV), F32),
            pltpu.VMEM((TOPK, KV), BF16),
            pltpu.VMEM((3, TOPK, 128), BF16),
            pltpu.VMEM((TOPK, 128), BF16),
            pltpu.VMEM((NZ, TOPK, 128), BF16),
            pltpu.VMEM((NQ, TOPK, 128), F32),
            dma((6,)),
            dma((9,)), dma((9,)),
            dma((2, SUBS)), dma((2, SUBS)),
            dma((2, 3, SUBS)), dma((2, 3, SUBS)),
            dma((2, NY)), dma((2, NY)),
            dma((2, 4, 2)), dma((2, 4, 2)),
            dma((2, 5, 2)), dma((2, 5, 2)),
            dma((3, 8)), dma((3, 8)),
        ],
        compiler_params=pltpu.CompilerParams(
            collective_id=0, has_side_effects=True, vmem_limit_bytes=40 << 20
        ),
        name="step",
    )(activations, cotangent, weight, momentum, positions, table)


def finish_kernel(table, mean, inv, given, moment, update, result, kept, dense, sem):
    copies = [pltpu.make_async_copy(given, result, sem.at[0]), pltpu.make_async_copy(moment, kept, sem.at[1])]
    for copy in copies:
        copy.start()
    for column in range(KV // 128):
        lanes = pl.ds(column * 128, 128)
        for r in range(SPAN // 8):
            dense[pl.ds(r * 8, 8), lanes] = pick_rows(mean[:, lanes], inv[pl.ds(r * 8, 8), lanes], TOPK // 8)
    update[...] = dot_full(table[...], dense[...], ((0,), (0,))).astype(BF16)
    for copy in copies:
        copy.wait()


def finish(table, mean, inv, given, moment):
    hbm, vmem = pl.BlockSpec(memory_space=pltpu.HBM), pl.BlockSpec(memory_space=pltpu.VMEM)
    return pl.pallas_call(
        finish_kernel,
        out_shape=(
            jax.ShapeDtypeStruct((SPAN, KV), BF16),
            jax.ShapeDtypeStruct((TOK, FEAT), BF16),
            jax.ShapeDtypeStruct((1, SPAN, KV), F32),
        ),
        in_specs=[vmem] * 5,
        out_specs=(vmem, hbm, hbm),
        scratch_shapes=[pltpu.VMEM((SPAN, KV), F32), pltpu.SemaphoreType.DMA((2,))],
        compiler_params=pltpu.CompilerParams(vmem_limit_bytes=8 << 20),
        name="finish",
    )(table, mean, inv, given, moment)


def on_device(activations, cotangent, weight, momentum, positions):
    table = jnp.asarray(transform_table(SPAN))
    held = [
        pltpu.with_memory_space_constraint(array, pltpu.HBM)
        for array in (activations, cotangent, weight.reshape(16, 16, KV), momentum[0], positions[0], table)
    ]
    moment, product, mean, inv = step(*held)
    update, grad_input, kept = finish(table, mean, inv, product, moment)
    return grad_input, kept, update


def solution(mesh):
    placed = (
        P(("dp", "fsdp"), None),
        P(("dp", "fsdp"), None),
        P("fsdp", None),
        P("dp", "fsdp", None),
        P("fsdp", None, None),
    )
    return jax.shard_map(
        on_device,
        mesh=mesh,
        in_specs=placed,
        out_specs=(P(("dp", "fsdp"), None), P("dp", "fsdp", None), P("fsdp", None)),
        check_vma=False,
    )
```

time: 281 us -> 64.6 us (0.23)
  waiting for transfers between devices: 235 us -> 0 us
  Pallas kernels: 0 us -> 63.6 us
  matrix products: 17.9 us -> 0 us
  between operations: 13.9 us -> 0.66 us
  other arithmetic: 9.54 us -> 0 us
  local copies, waits for them, and re-layouts: 2.94 us -> 0.01 us
    all_gather x2 -> x0, waiting for transfers between devices: 157 us -> none  [the longest x1 84.1 us: on_device(): lax.all_gather(bands[None], 'dp', axis=0, tiled=True).astype(jnp.float32)]
    reduce_scatter x1 -> x0, waiting for transfers between devices: 77.3 us -> none  [on_device(): lax.psum_scatter(lax.dot_general(activations, cotangent, (((0,), (0,)), (...]
    pallas_call x0 -> x2, Pallas kernels: none -> 63.6 us  [the longest x1 61.6 us: step(): pl.pallas_call(step_kernel, out_shape=(jax.ShapeDtypeStruct((1, SPAN, KV)...]
    dot_general x5 -> x0, matrix products: 17.9 us -> none  [the longest x2 5.26 us: inverse_blocks(): jnp.einsum('kn,bkc->bnc', table, coeffs, precision=lax.Precision.HIGHEST)]
    reduce_sum x13 -> x0, other arithmetic: 7.45 us -> none  [the longest x8 4.22 us: add_group(): jnp.sum(jnp.where(onehot, amounts[:, :, None, :], 0.0), axis=1)]
  transfers between devices with their start and end apart: 3 -> 0, of which waited for: 3 -> 0; matrix products, arithmetic and copies ran while one was open for 5% -> 0% of each run, Pallas kernels for 0% -> 0%
where the time goes in v2:
time: 64.6 us; the launch traced here: 64.3 us
  Pallas kernels  63.6 us (98%)
  between operations  0.66 us (1%)
    pallas_call x1, Pallas kernels, step(): pl.pallas_call(step_kernel, out_shape=(jax.ShapeDtypeStruct((1, SPAN, KV)...  61.6 us
    pallas_call x1, Pallas kernels, finish(): pl.pallas_call(finish_kernel, out_shape=(jax.ShapeDtypeStruct((SPAN, KV),...  2.05 us

profile of v2, /device:TPU:1, one launch (start us, length us, event | category | flops | bytes accessed | tf_op | source)
XLA Modules:
  0.0 64.3 jit_solution(5007763680206943861)
XLA Ops:
  0.6 0.0 copy-start
  0.6 61.6 %step.1 = (f32[1,256,512]{2,1,0:T(8,128)S(1)}, bf16[192,4096]{1,0:T(8,128)(2,1)S(1)}, f32[32,512]{1,0:T(8,128)S(1)}, s32[256,512]{1,0:T(8,128)S(1)}) custom-call(bf16[192,4096]{1,0:T(8,128)(2,1)} %a.1, bf16[192,512]{1,0:T(8,128)(2,1)} %c.1, bf16[16,16,512]{2,1,0:T(8,128)(2,1)} %bitcast.4, f32[256,512]{1,0:T(8,128)} %bitcast.3, s32[32,512]{1,0:T(8,128)} %bitcast.5, ...), custom_call_target="tpu_custom_call" | custom-call | tf_op jit(solution)/shard_map/step/pallas_call | solution.py:362
  62.2 0.0 copy-done
  62.2 2.1 %finish.1 = (bf16[256,512]{1,0:T(8,128)(2,1)}, bf16[192,4096]{1,0:T(8,128)(2,1)}, f32[1,256,512]{2,1,0:T(8,128)}) custom-call(f32[256,256]{1,0:T(8,128)S(1)} %copy-done, f32[32,512]{1,0:T(8,128)S(1)} %get-tuple-element.10.mean, s32[256,512]{1,0:T(8,128)S(1)} %get-tuple-element.11.inv, bf16[192,4096]{1,0:T(8,128)(2,1)S(1)} %get-tuple-element.12.given, ...), custom_call_target="tpu_custom_call" | custom-call | tf_op jit(solution)/shard_map/finish/pallas_call | solution.py:423
Async XLA Ops:
  0.6 61.6 %copy-start = (f32[256,256]{1,0:T(8,128)S(1)}, f32[256,256]{1,0:T(8,128)}, u32[]{:S(2)}) copy-start(f32[256,256]{1,0:T(8,128)} %constant.2.clone.table) | copy-start | bytes 786436

commit v3 on v2

--- a/solution.py
+++ b/solution.py
@@ -59,7 +59,7 @@
     kept, out, mean, inv,
     av, cv, pos, tv, mv, ax, cx, part, full, half_s, half_r, block_s, block_r,
     coeffs, bands, first, total, second, third,
-    ls, xs, xr, hs, hr, ys, yr, ws, wr, zs, zr, cs, cr, ss, sr,
+    ls, xs, xr, hs, hr, ys, yr, ws, wr, zs, zr, fs, fr, cs, cr, ss, sr,
 ):
     d, f = lax.axis_index("dp"), lax.axis_index("fsdp")
     x, y = f // NY, lax.rem(f, NY)
@@ -68,6 +68,7 @@
     piece = z * 2 + core
     other_x = lax.rem(f + NY, NX * NY)
     other_core = d + 1 - 2 * core
+    other_hi = z * NQ + (1 - hi) * 2 + core
 
     def wrap_y(at):
         return lax.rem(at + 2 * NY, NY)
@@ -98,9 +99,7 @@
         copy.start()
 
     meet(
-        [(d, other_x)]
-        + [(d, at_y(o)) for o in range(1, NY)]
-        + [(at_z(o), f) for o in range(1, NZ)]
+        [(d, other_x), (other_hi, other_x), (d, at_y(1)), (d, at_y(-1)), (at_z(1), f), (at_z(-1), f)]
         + [(z * NQ + at_q(k), f) for k in range(1, NQ)]
     )
 
@@ -111,20 +110,25 @@
         columns = pl.ds(pl.multiple_of((1 - x) * HALF + block * SPAN, SPAN), SPAN)
         return remote(a.at[:, columns], ax.at[block], xs.at[block], xr.at[block], d, other_x)
 
-    def own_piece(o):
-        target = other_x if o == 0 else at_y(o)
-        recv = wr.at[1, 0] if o == 0 else wr.at[0, o]
-        return remote(w.at[piece], full.at[f, piece], ws.at[0, o], recv, d, target)
-
-    def passed_piece(o):
-        ref = full.at[other_x, piece]
-        return remote(ref, ref, ws.at[1, o], wr.at[1, o], d, at_y(o))
+    def piece_copy(direction, step, arriving=0):
+        way = 1 - 2 * direction
+        ref = full.at[at_y(-(step + arriving) * way), piece]
+        first_hop = step == 0 and not arriving
+        return remote(
+            w.at[piece] if first_hop else ref, ref, ws.at[direction, step], wr.at[direction, step], d, at_y(way)
+        )
+
+    def pass_pieces(step):
+        for direction in range(2):
+            if step - 1 < 4 - direction:
+                piece_copy(direction, step - 1, arriving=1).wait_recv()
+            if step < 4 - direction:
+                piece_copy(direction, step).start()
 
     far_first = (4, 3, 5, 2, 6, 1, 7)
-    own_piece(0).start()
+    for direction in range(2):
+        piece_copy(direction, 0).start()
     cot_copy().start()
-    for o in far_first:
-        own_piece(o).start()
     for o in (4, 3, -3, 2, -2, 1, -1, 0):
         act_copy(wrap_y(y + o)).start()
 
@@ -140,10 +144,7 @@
             found = jnp.where(row == level, i, found)
         inv[rows, :] = found
 
-    passed = full.at[other_x, piece]
-    remote(w.at[piece], passed, ws.at[0, 0], wr.at[1, 0], d, other_x).wait_recv()
-    for o in far_first:
-        passed_piece(o).start()
+    pass_pieces(1)
 
     local[1].wait()
     local[2].wait()
@@ -152,6 +153,8 @@
     def _(block):
         columns = pl.ds(pl.multiple_of(block * SPAN, SPAN), SPAN)
         part[block] = lax.dot_general(av[:, columns], cv[...], TOKENS_IN, preferred_element_type=F32)
+
+    pass_pieces(2)
 
     def product(block):
         act_copy(block).wait_recv()
@@ -202,61 +205,73 @@
     def z_block(direction, step, which):
         return wrap_z(z - step * (1 - 2 * direction)) * 2 + which
 
+    def shards(side, sub):
+        return pl.ds(side * 8 + sub * 4, 4)
+
     def z_copy(direction, step, sub, arriving=0):
-        ref = full.at[pl.ds(sub * 8, 8), z_block(direction, step + arriving, core)]
+        ref = full.at[shards(x, sub), z_block(direction, step + arriving, core)]
         return remote(
             ref, ref, zs.at[direction, step, sub], zr.at[direction, step, sub], at_z(1 - 2 * direction), f
         )
 
-    def core_copy(direction, step, sub, which):
-        ref = full.at[pl.ds(sub * 8, 8), z_block(direction, step, which)]
-        return remote(ref, ref, cs.at[direction, step, sub], cr.at[direction, step, sub], other_core, f)
-
-    def halves_of(direction, step):
-        return (0, 1) if step < 3 else (direction,)
-
-    forwards = [(0, 0, 0), (0, 0, 1)] + [
-        (direction, step, sub)
-        for step in range(1, 5)
-        for direction in range(2)
-        for sub in halves_of(direction, step - 1)
-    ]
+    def far_copy(direction, step, sub, side):
+        ref = full.at[shards(side, sub), z_block(direction, step, core)]
+        return remote(
+            ref, ref, fs.at[direction, step, sub], fr.at[direction, step, sub], other_hi, other_x
+        )
+
+    def core_copy(far, direction, step, sub, which):
+        side = 1 - x if far else x
+        ref = full.at[shards(side, sub), z_block(direction, step, which)]
+        return remote(
+            ref, ref, cs.at[far, direction, step, sub], cr.at[far, direction, step, sub], other_core, f
+        )
+
+    def units(step):
+        if step == 0:
+            return ((0, 0), (0, 1))
+        if step == 4:
+            return ((0, 0), (1, 1))
+        return ((0, 0), (1, 0), (0, 1), (1, 1))
 
     def relay(step):
-        for direction in range(2):
-            for sub in halves_of(direction, step - 1):
+        if step == 0:
+            for sub in range(2):
+                for direction in range(2):
+                    z_copy(direction, 0, sub).start()
+        elif step < 5:
+            for direction, sub in units(step):
                 z_copy(direction, step - 1, sub, arriving=1).wait_recv()
-                if step < 4 and sub in halves_of(direction, step):
+                if step < 3 or (step == 3 and sub == direction):
                     z_copy(direction, step, sub).start()
-                core_copy(direction, step, sub, core).start()
-
+        if step < 5:
+            for direction, sub in units(step):
+                far_copy(direction, step, sub, x).start()
+                core_copy(0, direction, step, sub, core).start()
+        if step > 0:
+            for direction, sub in units(step - 1):
+                far_copy(direction, step - 1, sub, 1 - x).wait_recv()
+                core_copy(1, direction, step - 1, sub, core).start()
+
+    pass_pieces(3)
     cot_copy().wait_recv()
     product(wrap_y(y + 4))
     send_halves()
+    local[3].wait()
+    pass_pieces(4)
+    relay(0)
     for o in (3, -3):
         product(wrap_y(y + o))
     send_blocks(0)
-
-    local[3].wait()
-    for o in range(1, NY):
-        ref = full.at[at_y(-o), piece]
-        remote(ref, ref, ws.at[0, o], wr.at[0, o], d, at_y(o)).wait_recv()
-        ref = full.at[lax.rem(at_y(-o) + NY, NX * NY), piece]
-        remote(ref, ref, ws.at[1, o], wr.at[1, o], d, at_y(o)).wait_recv()
-    for direction in range(2):
-        for sub in range(2):
-            z_copy(direction, 0, sub).start()
-    for sub in range(2):
-        core_copy(0, 0, sub, core).start()
-
+    relay(1)
     for o in (2, -2):
         product(wrap_y(y + o))
     send_blocks(1)
-    relay(1)
+    relay(2)
     for o in (1, -1):
         product(wrap_y(y + o))
     send_blocks(2)
-    relay(2)
+    relay(3)
     product(y)
     local[5].wait()
     for sub in range(SUBS):
@@ -302,9 +317,10 @@
                 cv[...], rows, (((1,), (1,)), ((), ())), preferred_element_type=F32
             ).astype(BF16)
 
+    forwards = [(far, way, step, sub) for step in range(5) for far in range(2) for way, sub in units(step)]
     for k in (3, 2, 1):
         one(k).start()
-    relay(3)
+    relay(4)
     masked = jnp.where(inv[...] >= 0, coeffs[...], 0.0)
     kept[0] = mv[...] - dot_full(tv[...], masked, ((0,), (0,)))
     summed = bands[:, pl.ds(pl.multiple_of(q * 128, 128), 128)].astype(F32)
@@ -315,9 +331,9 @@
     for o in far_first:
         two(o).start()
     second[z] = summed.astype(BF16)
-    relay(4)
-    for direction, step, sub in forwards:
-        core_copy(direction, step, sub, 1 - core).wait_recv()
+    relay(5)
+    for far, direction, step, sub in forwards:
+        core_copy(far, direction, step, sub, 1 - core).wait_recv()
     grad_inputs(0, 5)
     for o in range(1, NZ):
         two_arrived(o).wait_recv()
@@ -336,19 +352,21 @@
     cot_copy().wait_send()
     for o in range(NY):
         act_copy(o).wait_send()
-        own_piece(o).wait_send()
-    for o in range(1, NY):
-        passed_piece(o).wait_send()
     for direction in range(2):
         for sub in range(SUBS):
             half_copy(direction, sub).wait_send()
             for step in range(3):
                 block_copy(direction, step, sub).wait_send()
         for step in range(4):
-            for sub in halves_of(direction, step):
-                z_copy(direction, step, sub).wait_send()
-    for direction, step, sub in forwards:
-        core_copy(direction, step, sub, core).wait_send()
+            if step < 4 - direction:
+                piece_copy(direction, step).wait_send()
+            for sub in range(2):
+                if step < 3 or sub == direction:
+                    z_copy(direction, step, sub).wait_send()
+    for far, direction, step, sub in forwards:
+        core_copy(far, direction, step, sub, core).wait_send()
+        if far:
+            far_copy(direction, step, sub, x).wait_send()
     for k in range(1, NQ):
         one(k).wait_send()
         three(k).wait_send()
@@ -393,9 +411,10 @@
             dma((9,)), dma((9,)),
             dma((2, SUBS)), dma((2, SUBS)),
             dma((2, 3, SUBS)), dma((2, 3, SUBS)),
-            dma((2, NY)), dma((2, NY)),
+            dma((2, 4)), dma((2, 4)),
             dma((2, 4, 2)), dma((2, 4, 2)),
             dma((2, 5, 2)), dma((2, 5, 2)),
+            dma((2, 2, 5, 2)), dma((2, 2, 5, 2)),
             dma((3, 8)), dma((3, 8)),
         ],
         compiler_params=pltpu.CompilerParams(

time: 64.6 us -> 64 us (level)
  no operation moved by 1% of the time
where the time goes in v3:
time: 64 us; the launch traced here: 63.9 us
  Pallas kernels  63.3 us (99%)
  between operations  0.66 us (1%)
    pallas_call x1, Pallas kernels, step(): pl.pallas_call(step_kernel, out_shape=(jax.ShapeDtypeStruct((1, SPAN, KV)...  61.2 us
    pallas_call x1, Pallas kernels, finish(): pl.pallas_call(finish_kernel, out_shape=(jax.ShapeDtypeStruct((SPAN, KV),...  2.05 us

profile of v3, /device:TPU:1, one launch (start us, length us, event | category | flops | bytes accessed | tf_op | source)
XLA Modules:
  0.0 63.9 jit_solution(7614932696055079415)
XLA Ops:
  0.6 0.0 copy-start
  0.6 61.2 %step.1 = (f32[1,256,512]{2,1,0:T(8,128)S(1)}, bf16[192,4096]{1,0:T(8,128)(2,1)S(1)}, f32[32,512]{1,0:T(8,128)S(1)}, s32[256,512]{1,0:T(8,128)S(1)}) custom-call(bf16[192,4096]{1,0:T(8,128)(2,1)} %a.1, bf16[192,512]{1,0:T(8,128)(2,1)} %c.1, bf16[16,16,512]{2,1,0:T(8,128)(2,1)} %bitcast.4, f32[256,512]{1,0:T(8,128)} %bitcast.3, s32[32,512]{1,0:T(8,128)} %bitcast.5, ...), custom_call_target="tpu_custom_call" | custom-call | tf_op jit(solution)/shard_map/step/pallas_call | solution.py:380
  61.9 0.0 copy-done
  61.9 2.1 %finish.1 = (bf16[256,512]{1,0:T(8,128)(2,1)}, bf16[192,4096]{1,0:T(8,128)(2,1)}, f32[1,256,512]{2,1,0:T(8,128)}) custom-call(f32[256,256]{1,0:T(8,128)S(1)} %copy-done, f32[32,512]{1,0:T(8,128)S(1)} %get-tuple-element.10.mean, s32[256,512]{1,0:T(8,128)S(1)} %get-tuple-element.11.inv, bf16[192,4096]{1,0:T(8,128)(2,1)S(1)} %get-tuple-element.12.given, ...), custom_call_target="tpu_custom_call" | custom-call | tf_op jit(solution)/shard_map/finish/pallas_call | solution.py:442
Async XLA Ops:
  0.6 61.2 %copy-start = (f32[256,256]{1,0:T(8,128)S(1)}, f32[256,256]{1,0:T(8,128)}, u32[]{:S(2)}) copy-start(f32[256,256]{1,0:T(8,128)} %constant.2.clone.table) | copy-start | bytes 786436

commit v4 on v3

--- a/solution.py
+++ b/solution.py
@@ -274,22 +274,14 @@
     relay(3)
     product(y)
     local[5].wait()
+    mv[...] = MOMENTUM_DECAY * mv[...] + part[y]
     for sub in range(SUBS):
         rows = pl.ds(sub * rows_of, rows_of)
-        gradient = part[y, rows, :]
+        moment = mv[rows, :]
         for direction in range(2):
             block_copy(direction, 2, sub).wait_recv()
-            gradient = gradient + block_r[direction, 2, rows].astype(F32)
-        mv[rows, :] = MOMENTUM_DECAY * mv[rows, :] + gradient
-
-    local[4].wait()
-    coeffs[...] = dot_full(tv[...], mv[...], ((1,), (0,)))
-    for column in range(KV // 128):
-        lanes = pl.ds(column * 128, 128)
-        picked = [
-            pick_rows(coeffs[:, lanes], pos[pl.ds(r * 8, 8), lanes], SPAN // 8) for r in range(TOPK // 8)
-        ]
-        bands[:, lanes] = jnp.concatenate(picked, axis=0).astype(BF16)
+            moment = moment + block_r[direction, 2, rows].astype(F32)
+        mv[rows, :] = moment
 
     def one(k):
         columns = pl.ds(pl.multiple_of(at_q(k) * 128, 128), 128)
@@ -308,9 +300,10 @@
         slot = third.at[at_q(k)]
         return remote(slot, slot, ss.at[2, k], sr.at[2, k], z * NQ + at_q(k), f)
 
-    def grad_inputs(low, high):
-        @pl.loop(low, high)
-        def _(tile):
+    def grad_inputs(side):
+        @pl.loop(0, 4)
+        def _(at):
+            tile = side * 4 + at
             columns = pl.ds(pl.multiple_of(tile * 512, 512), 512)
             rows = full[pl.ds(tile * 2, 2)].reshape(512, KV)
             out[:, columns] = lax.dot_general(
@@ -318,8 +311,18 @@
             ).astype(BF16)
 
     forwards = [(far, way, step, sub) for step in range(5) for far in range(2) for way, sub in units(step)]
-    for k in (3, 2, 1):
-        one(k).start()
+    local[4].wait()
+    for to in ((3, 2), (1, 0)):
+        side = pl.ds(pl.multiple_of(at_q(to[1]) // 2 * SPAN, SPAN), SPAN)
+        coeffs[:, side] = dot_full(tv[...], mv[:, side], ((1,), (0,)))
+        for k in to:
+            lanes = pl.ds(pl.multiple_of(at_q(k) * 128, 128), 128)
+            picked = [
+                pick_rows(coeffs[:, lanes], pos[pl.ds(r * 8, 8), lanes], SPAN // 8) for r in range(TOPK // 8)
+            ]
+            bands[:, lanes] = jnp.concatenate(picked, axis=0).astype(BF16)
+            if k:
+                one(k).start()
     relay(4)
     masked = jnp.where(inv[...] >= 0, coeffs[...], 0.0)
     kept[0] = mv[...] - dot_full(tv[...], masked, ((0,), (0,)))
@@ -331,23 +334,27 @@
     for o in far_first:
         two(o).start()
     second[z] = summed.astype(BF16)
-    relay(5)
     for far, direction, step, sub in forwards:
-        core_copy(far, direction, step, sub, 1 - core).wait_recv()
-    grad_inputs(0, 5)
+        if not far:
+            core_copy(far, direction, step, sub, 1 - core).wait_recv()
+    grad_inputs(x)
     for o in range(1, NZ):
         two_arrived(o).wait_recv()
     summed = second[0].astype(F32)
     for at in range(1, NZ):
         summed = summed + second[at].astype(F32)
-    third[q] = summed / (NZ * NQ)
+    third[q] = (summed / (NZ * NQ)).astype(BF16)
     for k in (3, 2, 1):
         three(k).start()
-    grad_inputs(5, 8)
+    relay(5)
+    for far, direction, step, sub in forwards:
+        if far:
+            core_copy(far, direction, step, sub, 1 - core).wait_recv()
+    grad_inputs(1 - x)
     for k in range(1, NQ):
         three_arrived(k).wait_recv()
     for at in range(NQ):
-        mean[:, at * 128 : at * 128 + 128] = third[at]
+        mean[:, at * 128 : at * 128 + 128] = third[at].astype(F32)
 
     cot_copy().wait_send()
     for o in range(NY):
@@ -406,7 +413,7 @@
             pltpu.VMEM((3, TOPK, 128), BF16),
             pltpu.VMEM((TOPK, 128), BF16),
             pltpu.VMEM((NZ, TOPK, 128), BF16),
-            pltpu.VMEM((NQ, TOPK, 128), F32),
+            pltpu.VMEM((NQ, TOPK, 128), BF16),
             dma((6,)),
             dma((9,)), dma((9,)),
             dma((2, SUBS)), dma((2, SUBS)),
@@ -424,15 +431,21 @@
     )(activations, cotangent, weight, momentum, positions, table)
 
 
-def finish_kernel(table, mean, inv, given, moment, update, result, kept, dense, sem):
+def finish_kernel(table, mean, inv, given, moment, update, result, kept, dense, decoded, sem):
     copies = [pltpu.make_async_copy(given, result, sem.at[0]), pltpu.make_async_copy(moment, kept, sem.at[1])]
     for copy in copies:
         copy.start()
-    for column in range(KV // 128):
-        lanes = pl.ds(column * 128, 128)
-        for r in range(SPAN // 8):
-            dense[pl.ds(r * 8, 8), lanes] = pick_rows(mean[:, lanes], inv[pl.ds(r * 8, 8), lanes], TOPK // 8)
-    update[...] = dot_full(table[...], dense[...], ((0,), (0,))).astype(BF16)
+    for half in range(2):
+        side = pl.ds(half * SPAN, SPAN)
+        for column in range(2):
+            lanes = pl.ds(half * SPAN + column * 128, 128)
+            for r in range(SPAN // 8):
+                dense[half, pl.ds(r * 8, 8), pl.ds(column * 128, 128)] = pick_rows(
+                    mean[:, lanes], inv[pl.ds(r * 8, 8), lanes], TOPK // 8
+                )
+        decoded[half] = dot_full(table[...], dense[half], ((0,), (0,))).astype(BF16)
+        copies.append(pltpu.make_async_copy(decoded.at[half], update.at[:, side], sem.at[2 + half]))
+        copies[-1].start()
     for copy in copies:
         copy.wait()
 
@@ -447,8 +460,12 @@
             jax.ShapeDtypeStruct((1, SPAN, KV), F32),
         ),
         in_specs=[vmem] * 5,
-        out_specs=(vmem, hbm, hbm),
-        scratch_shapes=[pltpu.VMEM((SPAN, KV), F32), pltpu.SemaphoreType.DMA((2,))],
+        out_specs=(hbm, hbm, hbm),
+        scratch_shapes=[
+            pltpu.VMEM((2, SPAN, SPAN), F32),
+            pltpu.VMEM((2, SPAN, SPAN), BF16),
+            pltpu.SemaphoreType.DMA((4,)),
+        ],
         compiler_params=pltpu.CompilerParams(vmem_limit_bytes=8 << 20),
         name="finish",
     )(table, mean, inv, given, moment)

time: 64 us -> 63.5 us (level)
  no operation moved by 1% of the time
where the time goes in v4:
time: 63.5 us; the launch traced here: 63.4 us
  Pallas kernels  62.8 us (99%)
  between operations  0.66 us (1%)
    pallas_call x1, Pallas kernels, step(): pl.pallas_call(step_kernel, out_shape=(jax.ShapeDtypeStruct((1, SPAN, KV)...  61.1 us
    pallas_call x1, Pallas kernels, finish(): pl.pallas_call(finish_kernel, out_shape=(jax.ShapeDtypeStruct((SPAN, KV),...  1.67 us

profile of v4, /device:TPU:1, one launch (start us, length us, event | category | flops | bytes accessed | tf_op | source)
XLA Modules:
  0.0 63.4 jit_solution(16654772375316972284)
XLA Ops:
  0.6 0.0 copy-start
  0.6 61.1 %step.1 = (f32[1,256,512]{2,1,0:T(8,128)S(1)}, bf16[192,4096]{1,0:T(8,128)(2,1)S(1)}, f32[32,512]{1,0:T(8,128)S(1)}, s32[256,512]{1,0:T(8,128)S(1)}) custom-call(bf16[192,4096]{1,0:T(8,128)(2,1)} %a.1, bf16[192,512]{1,0:T(8,128)(2,1)} %c.1, bf16[16,16,512]{2,1,0:T(8,128)(2,1)} %bitcast.4, f32[256,512]{1,0:T(8,128)} %bitcast.3, s32[32,512]{1,0:T(8,128)} %bitcast.5, ...), custom_call_target="tpu_custom_call" | custom-call | tf_op jit(solution)/shard_map/step/pallas_call | solution.py:387
  61.8 0.0 copy-done
  61.8 1.7 %finish.1 = (bf16[256,512]{1,0:T(8,128)(2,1)}, bf16[192,4096]{1,0:T(8,128)(2,1)}, f32[1,256,512]{2,1,0:T(8,128)}) custom-call(f32[256,256]{1,0:T(8,128)S(1)} %copy-done, f32[32,512]{1,0:T(8,128)S(1)} %get-tuple-element.10.mean, s32[256,512]{1,0:T(8,128)S(1)} %get-tuple-element.11.inv, bf16[192,4096]{1,0:T(8,128)(2,1)S(1)} %get-tuple-element.12.given, ...), custom_call_target="tpu_custom_call" | custom-call | tf_op jit(solution)/shard_map/finish/pallas_call | solution.py:455
Async XLA Ops:
  0.6 61.1 %copy-start = (f32[256,256]{1,0:T(8,128)S(1)}, f32[256,256]{1,0:T(8,128)}, u32[]{:S(2)}) copy-start(f32[256,256]{1,0:T(8,128)} %constant.2.clone.table) | copy-start | bytes 786436

commit v5 on v4

--- a/solution.py
+++ b/solution.py
@@ -324,8 +324,6 @@
             if k:
                 one(k).start()
     relay(4)
-    masked = jnp.where(inv[...] >= 0, coeffs[...], 0.0)
-    kept[0] = mv[...] - dot_full(tv[...], masked, ((0,), (0,)))
     summed = bands[:, pl.ds(pl.multiple_of(q * 128, 128), 128)].astype(F32)
     for k in range(1, NQ):
         one(k).wait_recv()
@@ -334,6 +332,8 @@
     for o in far_first:
         two(o).start()
     second[z] = summed.astype(BF16)
+    masked = jnp.where(inv[...] >= 0, coeffs[...], 0.0)
+    kept[0] = mv[...] - dot_full(tv[...], masked, ((0,), (0,)))
     for far, direction, step, sub in forwards:
         if not far:
             core_copy(far, direction, step, sub, 1 - core).wait_recv()

time: 63.5 us -> 63.3 us (level)
  no operation moved by 1% of the time
where the time goes in v5:
time: 63.3 us; the launch traced here: 63.2 us
  Pallas kernels  62.5 us (99%)
  between operations  0.66 us (1%)
    pallas_call x1, Pallas kernels, step(): pl.pallas_call(step_kernel, out_shape=(jax.ShapeDtypeStruct((1, SPAN, KV)...  60.9 us
    pallas_call x1, Pallas kernels, finish(): pl.pallas_call(finish_kernel, out_shape=(jax.ShapeDtypeStruct((SPAN, KV),...  1.67 us

profile of v5, /device:TPU:1, one launch (start us, length us, event | category | flops | bytes accessed | tf_op | source)
XLA Modules:
  0.0 63.2 jit_solution(12039786950119735869)
XLA Ops:
  0.6 0.0 copy-start
  0.6 60.9 %step.1 = (f32[1,256,512]{2,1,0:T(8,128)S(1)}, bf16[192,4096]{1,0:T(8,128)(2,1)S(1)}, f32[32,512]{1,0:T(8,128)S(1)}, s32[256,512]{1,0:T(8,128)S(1)}) custom-call(bf16[192,4096]{1,0:T(8,128)(2,1)} %a.1, bf16[192,512]{1,0:T(8,128)(2,1)} %c.1, bf16[16,16,512]{2,1,0:T(8,128)(2,1)} %bitcast.4, f32[256,512]{1,0:T(8,128)} %bitcast.3, s32[32,512]{1,0:T(8,128)} %bitcast.5, ...), custom_call_target="tpu_custom_call" | custom-call | tf_op jit(solution)/shard_map/step/pallas_call | solution.py:387
  61.5 0.0 copy-done
  61.5 1.7 %finish.1 = (bf16[256,512]{1,0:T(8,128)(2,1)}, bf16[192,4096]{1,0:T(8,128)(2,1)}, f32[1,256,512]{2,1,0:T(8,128)}) custom-call(f32[256,256]{1,0:T(8,128)S(1)} %copy-done, f32[32,512]{1,0:T(8,128)S(1)} %get-tuple-element.10.mean, s32[256,512]{1,0:T(8,128)S(1)} %get-tuple-element.11.inv, bf16[192,4096]{1,0:T(8,128)(2,1)S(1)} %get-tuple-element.12.given, ...), custom_call_target="tpu_custom_call" | custom-call | tf_op jit(solution)/shard_map/finish/pallas_call | solution.py:455
Async XLA Ops:
  0.6 60.9 %copy-start = (f32[256,256]{1,0:T(8,128)S(1)}, f32[256,256]{1,0:T(8,128)}, u32[]{:S(2)}) copy-start(f32[256,256]{1,0:T(8,128)} %constant.2.clone.table) | copy-start | bytes 786436
